TPU v7x, 256 devices: a whole 4x4x8 slice. The times are simulated.
256 devices in a mesh: sub: 32 (over x, z), vec: 8 (over y, core).
Axes of the slice: x: 4, y: 4, z: 8, core: 2. Of those that a mesh axis runs over, the one named last changes fastest.
Arguments:
- coefficients: bfloat16 [1024, 20480], P('sub', 'vec'), may hold values from -6 to 6
- row_counts: int32 [32], replicated, may hold values from 1 to 1024, 16384 in all
- ancestors: int32 [32, 3], replicated, may hold values from 0 to 27, as said below
- interior_modes: bfloat16 [131072, 1024], P('sub'), may hold values from -0.25 to 0.25
- separator_modes: bfloat16 [8192, 128], replicated, may hold values from -0.5 to 0.5
- coupling: bfloat16 [131072, 768], P('sub'), may hold values from -0.3125 to 0.3125
- pattern: int32 [32, 16, 3], P('sub'), may hold values 0 or 1
Outputs:
- interior_field: bfloat16 [131072, 1024], P('sub', 'vec')
- separator_field: bfloat16 [8192, 1024], P('sub', 'vec')
Inputs may be any that keep to these rules, and one draw needn't show every extreme that they name: `ancestors`: the separators form binary trees: substructures pair under level-1 separators, pairs of those under level-2 separators, and so on, so that a level-l separator lies over 2**l substructures; no separator appears at two levels. `row_counts`: the counts sum to 512 * 32.
All inputs are finite; a program needn't handle non-finite values. No bound on the sum of `pattern` on one device may be relied on, other than what follows from the above.
Results may differ from a plain program's by a relative error of at most 0.0038.
Values may be sent and summed in bfloat16 or wider, within the bound.
A program may use at most 128 MiB of HBM per device.

v0:
```python
import jax
import jax.numpy as jnp
from jax import lax
from jax.sharding import PartitionSpec as P

BW = 256
SEPM = 128
LEVELS = 3


def window_rows(full_rows, row_counts, interior_total, cap_rows):
    slice_cols = full_rows.shape[0]
    block_total = interior_total // cap_rows + 1
    padded = jnp.concatenate(
        [full_rows[:, :interior_total], jnp.zeros((slice_cols, cap_rows), full_rows.dtype)], axis=1
    )
    blocks = padded.reshape(slice_cols, block_total, cap_rows)
    offsets = jnp.cumsum(row_counts) - row_counts
    first_block = offsets // cap_rows
    remainder = offsets - first_block * cap_rows
    labels = jnp.arange(block_total, dtype=jnp.int32)
    pick_first = (first_block[:, None] == labels[None, :]).astype(blocks.dtype)
    pick_second = (first_block[:, None] + 1 == labels[None, :]).astype(blocks.dtype)
    lower = jnp.einsum("ob,cbj->ocj", pick_first, blocks, preferred_element_type=jnp.float32)
    upper = jnp.einsum("ob,cbj->ocj", pick_second, blocks, preferred_element_type=jnp.float32)
    window = jnp.concatenate([lower, upper], axis=2).astype(blocks.dtype)
    for bit in range(cap_rows.bit_length() - 1):
        amount = 1 << bit
        moved = jnp.concatenate(
            [window[:, :, amount:], jnp.zeros(window.shape[:2] + (amount,), window.dtype)], axis=2
        )
        flag = remainder >> bit & 1 == 1
        window = jnp.where(flag[:, None, None], moved, window)
    window = window[:, :, :cap_rows]
    positions = jnp.arange(cap_rows, dtype=jnp.int32)
    live = positions[None, :] < row_counts[:, None]
    window = jnp.where(live[:, None, :], window, jnp.zeros((), window.dtype))
    return jnp.transpose(window, (1, 0, 2))


def body(coefficients, row_counts, ancestors, interior_modes, separator_modes, coupling, pattern):
    sub_count = lax.axis_size("sub")
    vec_count = lax.axis_size("vec")
    my_index = lax.axis_index("sub")
    slice_cols = coefficients.shape[0] // vec_count
    rows_vec = coefficients.shape[1]
    regrouped = coefficients.reshape(vec_count, slice_cols, rows_vec)
    full_rows = lax.all_to_all(regrouped, "vec", split_axis=0, concat_axis=2, tiled=True)
    full_rows = full_rows.reshape(slice_cols, vec_count * rows_vec)
    total_rows = full_rows.shape[1]
    interior_total = total_rows - sub_count * SEPM
    cap_rows = interior_modes.shape[1]
    interior_part = window_rows(full_rows, row_counts, interior_total, cap_rows)
    sep_part = full_rows[:, interior_total:].reshape(slice_cols, sub_count, SEPM)
    parts = [interior_part, sep_part]
    picked = jnp.concatenate(parts, axis=2)
    slot_width = picked.shape[2]
    received = lax.all_to_all(picked, "sub", split_axis=1, concat_axis=0, tiled=True)
    group_cols = sub_count * slice_cols
    received = received.reshape(group_cols, slot_width)
    interior_coef = received[:, :cap_rows]
    own_coef = received[:, cap_rows : cap_rows + SEPM]
    modes_by_sep = separator_modes.reshape(sub_count, BW, SEPM)
    own_modes = lax.dynamic_index_in_dim(modes_by_sep, my_index, 0, keepdims=False)
    contract = (((1,), (1,)), ((), ()))
    own_field = lax.dot_general(
        own_modes, own_coef, contract, preferred_element_type=jnp.float32
    ).astype(jnp.bfloat16)
    interior_sum = lax.dot_general(
        interior_modes, interior_coef, contract, preferred_element_type=jnp.float32
    )
    my_ancestors = lax.dynamic_index_in_dim(ancestors, my_index, 0, keepdims=False)
    piece = lax.all_gather(own_field[None], "sub", axis=0, tiled=True)
    labels = jnp.arange(piece.shape[0], dtype=jnp.int32)
    select = (my_ancestors[:, None] == labels[None, :]).astype(piece.dtype)
    ancestor_blocks = jnp.einsum(
        "lc,cbk->lbk", select, piece, preferred_element_type=jnp.float32
    ).astype(jnp.bfloat16)
    block_count = coupling.shape[0] // BW
    gates = pattern[0].astype(coupling.dtype)
    masked = (coupling.reshape(block_count, BW, LEVELS, BW) * gates[:, None, :, None]).reshape(
        coupling.shape
    )
    interior_sum = interior_sum + jnp.dot(
        masked, ancestor_blocks.reshape(LEVELS * BW, group_cols), preferred_element_type=jnp.float32
    )
    return (interior_sum.astype(jnp.bfloat16), own_field)


def solution(mesh):
    placed = (P("sub", "vec"), P(), P(), P("sub", None), P(), P("sub", None), P("sub", None, None))
    return jax.shard_map(
        body,
        mesh=mesh,
        in_specs=placed,
        out_specs=(P("sub", "vec"), P("sub", "vec")),
        check_vma=False,
    )
```

profile of v0, /device:TPU:8, one launch (start us, length us, event | category | flops | bytes accessed | tf_op | source)
XLA Modules:
  0.0 143.3 jit_solution(3298135842300496320)
XLA Ops:
  7.2 0.0 copy-start
  7.2 1.8 %reshape.96 = bf16[8,4,2560]{2,1,0:T(4,128)(2,1)} reshape(bf16[32,2560]{1,0:T(8,128)(2,1)} %param.7) | data formatting | bytes 327680 | tf_op jit(solution)/shard_map/reshape | solution.py:47
  9.0 5.4 %all-to-all-start = ((bf16[8,4,2560]{2,1,0:T(4,128)(2,1)}), bf16[8,4,2560]{2,1,0:T(4,128)(2,1)S(1)}, u32[]{:S(2)}, u32[]{:S(2)}) async-start(bf16[8,4,2560]{2,1,0:T(4,128)(2,1)} %reshape.96), calls=%async_computation | async-start | bytes 327680 | tf_op jit(solution)/shard_map/all_to_all | solution.py:48
  14.4 0.7 iota_compare_fusion
  15.1 0.7 copy.21
  15.9 0.1 reduce-window.9
  15.9 0.1 reduce
  16.1 0.7 and_compare_fusion.9
  16.8 2.7 %all-to-all-done = bf16[8,4,2560]{2,1,0:T(4,128)(2,1)S(1)} async-done(((bf16[8,4,2560]{2,1,0:T(4,128)(2,1)}), bf16[8,4,2560]{2,1,0:T(4,128)(2,1)S(1)}, u32[]{:S(2)}, u32[]{:S(2)}) %all-to-all-start) | async-done | bytes 163872 | tf_op jit(solution)/shard_map/all_to_all | solution.py:48
  19.4 0.8 slice_select_fusion.1
  20.3 0.1 reshape.98
  20.4 0.3 convolution_convert_fusion.1
  20.7 0.3 convolution_convert_fusion
  20.9 0.2 fusion.9
  21.2 0.2 fusion.10
  21.4 0.2 slice.64
  21.6 0.2 pad_select_fusion.7
  21.8 0.2 slice.65
  22.0 0.2 pad_select_fusion.6
  22.2 0.2 slice.66
  22.4 0.2 pad_select_fusion.5
  22.7 0.2 slice.67
  22.9 0.2 pad_select_fusion.4
  23.1 0.2 slice.68
  23.3 0.2 pad_select_fusion.3
  23.5 0.0 copy-start.1
  23.5 0.0 copy-start.2
  23.5 0.2 slice.69
  23.7 0.2 pad_select_fusion.2
  24.0 0.2 pad_select_fusion.1
  24.2 0.2 pad_select_fusion
  24.5 0.2 fusion.13
  24.7 0.9 copy.22
  25.5 10.7 %all-to-all-start.1 = ((bf16[4,32,1152]{2,0,1:T(4,128)(2,1)}), bf16[4,32,1152]{2,0,1:T(4,128)(2,1)S(1)}, u32[]{:S(2)}, u32[]{:S(2)}) async-start(bf16[4,32,1152]{2,0,1:T(4,128)(2,1)} %copy.22), calls=%async_computation.1 | async-start | bytes 589824 | tf_op jit(solution)/shard_map/all_to_all | solution.py:58
  36.3 0.2 all-gather.3.cloned.1.call-start
  36.5 12.5 %all-to-all-done.1 = bf16[4,32,1152]{2,0,1:T(4,128)(2,1)S(1)} async-done(((bf16[4,32,1152]{2,0,1:T(4,128)(2,1)}), bf16[4,32,1152]{2,0,1:T(4,128)(2,1)S(1)}, u32[]{:S(2)}, u32[]{:S(2)}) %all-to-all-start.1) | async-done | bytes 294944 | tf_op jit(solution)/shard_map/all_to_all | solution.py:58
  49.0 0.1 reshape.100
  49.1 0.0 copy-done
  49.1 0.8 convolution_convert_fusion.2
  49.9 0.0 all-gather.3.cloned.1.call-update
  49.9 0.0 copy-done.1
  49.9 0.2 dynamic-slice_reduce_fusion
  50.1 0.0 copy-done.2
  50.1 0.5 mul.16
  50.6 6.8 %copy.31 = bf16[96,8,16,256]{3,1,2,0:T(8,128)(2,1)} copy(bf16[96,8,16,256]{3,2,1,0:T(8,128)(2,1)S(1)} %bitcast.53) | data formatting | bytes 12582912
  57.5 8.8 %copy.23 = bf16[4096,768]{0,1:T(8,128)(2,1)} copy(bf16[4096,768]{1,0:T(8,128)(2,1)} %param.12) | data formatting | bytes 12582912 | tf_op args[5]
  66.2 56.9 %all-gather.3.cloned.1.call-done = bf16[8192,128]{1,0:T(8,128)(2,1)} async-done(((bf16[256,128]{1,0:T(8,128)(2,1)}), bf16[8192,128]{1,0:T(8,128)(2,1)}) %all-gather.3.cloned.1.call-update) | async-done | bytes 2097168 | tf_op jit(solution)/shard_map/all_gather | solution.py:73
  123.1 0.0 slice-start
  123.1 3.0 %fusion.6 = bf16[3,256,128]{2,0,1:T(4,128)(2,1)S(1)} fusion(bf16[32,256,128]{2,1,0:T(8,128)(2,1)} %bitcast.56, s32[3]{0:T(128)S(1)} %dynamic-slice_reduce_fusion), kind=kOutput, calls=%fused_computation.9 | convolution fusion | flops 6389856 | bytes 2293772 | tf_op jit(solution)/shard_map/lc,cbk->lbk/dot_general | solution.py:76
  126.1 0.0 slice-start.1
  126.1 6.1 %fusion = f32[4096,128]{0,1:T(8,128)S(1)} fusion(bf16[768,128]{1,0:T(8,128)(2,1)S(1)} %bitcast.58, bf16[4096,768]{0,1:T(8,128)(2,1)} %copy.23, bf16[4096,768]{0,1:T(8,128)(2,1)} %bitcast.52), kind=kOutput, calls=%fused_computation | convolution fusion | flops 808452096 | bytes 14876672 | tf_op jit(solution)/shard_map/dot_general | solution.py:84
  132.2 0.0 slice-done
  132.2 0.0 slice-done.1
  132.2 2.9 %fusion.3 = bf16[4096,128]{0,1:T(8,128)(2,1)S(1)} fusion(f32[4096,128]{0,1:T(8,128)S(1)} %fusion, bf16[4096,1024]{1,0:T(8,128)(2,1)S(1)} %bitcast.55, bf16[128,1152]{1,0:T(8,128)(2,1)S(1)} %reshape.100), kind=kOutput, calls=%fused_computation.4 | convolution fusion | flops 1074790400 | bytes 11796480 | tf_op jit(solution)/shard_map/dot_general | solution.py:69
  135.1 1.3 copy.27
  (12 shorter events, 0.2 us)
Async XLA Ops:
  7.2 41.9 %copy-start = (bf16[8192,128]{1,0:T(8,128)(2,1)S(1)}, bf16[8192,128]{1,0:T(8,128)(2,1)}, u32[]{:S(2)}) copy-start(bf16[8192,128]{1,0:T(8,128)(2,1)} %param.11) | copy-start | bytes 6291460
  9.0 10.5 %all-to-all-start = ((bf16[8,4,2560]{2,1,0:T(4,128)(2,1)}), bf16[8,4,2560]{2,1,0:T(4,128)(2,1)S(1)}, u32[]{:S(2)}, u32[]{:S(2)}) async-start(bf16[8,4,2560]{2,1,0:T(4,128)(2,1)} %reshape.96), calls=%async_computation | async-start | bytes 327680 | tf_op jit(solution)/shard_map/all_to_all | solution.py:48
  23.5 26.4 %copy-start.1 = (s32[32,3]{0,1:T(4,128)S(1)}, s32[32,3]{0,1:T(4,128)}, u32[]{:S(2)}) copy-start(s32[32,3]{0,1:T(4,128)} %param.9) | copy-start | bytes 1156
  23.5 26.6 %copy-start.2 = (s32[1,16,3]{1,0,2:T(1,128)S(1)}, s32[1,16,3]{1,0,2:T(1,128)}, u32[]{:S(2)}) copy-start(s32[1,16,3]{1,0,2:T(1,128)} %param.13) | copy-start | bytes 580
  25.5 23.5 %all-to-all-start.1 = ((bf16[4,32,1152]{2,0,1:T(4,128)(2,1)}), bf16[4,32,1152]{2,0,1:T(4,128)(2,1)S(1)}, u32[]{:S(2)}, u32[]{:S(2)}) async-start(bf16[4,32,1152]{2,0,1:T(4,128)(2,1)} %copy.22), calls=%async_computation.1 | async-start | bytes 589824 | tf_op jit(solution)/shard_map/all_to_all | solution.py:58
  36.3 86.8 %all-gather.3.cloned.1.call-start = ((), (), s32[]{:S(2)}) async-start(), calls=%async_computation.2 | async-start | bytes 2162688 | tf_op jit(solution)/shard_map/all_gather | solution.py:73
  123.1 9.1 %slice-start = ((s8[8388608]{0:T(1024)(128)(4,1)}), s8[4194304]{0:T(1024)(128)(4,1)S(1)}, s32[]{:S(2)}) async-start(s8[8388608]{0:T(1024)(128)(4,1)} %bitcast.54), calls=%async_computation.3 | async-start | bytes 8388608
  126.1 6.1 %slice-start.1 = ((s8[8388608]{0:T(1024)(128)(4,1)}), s8[4194304]{0:T(1024)(128)(4,1)S(1)}, s32[]{:S(2)}) async-start(s8[8388608]{0:T(1024)(128)(4,1)} %bitcast.54), calls=%async_computation.4 | async-start | bytes 8388608
Sparse Core Ops, SparseCore 0:
  50.0 72.9 all-gather.2
where the time goes:
time: 144 us; the launch traced here: 143 us
  waiting for transfers between devices  72 us (50%)
  local copies, waits for them, and re-layouts  22.5 us (16%)
  starting transfers between devices  16.4 us (11%)
  between operations  14.4 us (10%)
  matrix products  13.3 us (9%)
  other arithmetic  4.63 us (3%)
    all_gather x1, waiting for transfers between devices, body(): piece = lax.all_gather(own_field[None], 'sub', axis=0, tiled=True)  56.9 us
    unnamed x16, local copies, waits for them, and re-layouts  17 us
    all_to_all x1, waiting for transfers between devices, body(): lax.all_to_all(picked, 'sub', split_axis=1, concat_axis=0, tiled=True)  12.5 us
    all_to_all x1, starting transfers between devices, body(): lax.all_to_all(picked, 'sub', split_axis=1, concat_axis=0, tiled=True)  10.7 us
    dot_general x1, matrix products, body(): jnp.dot(masked, ancestor_blocks.reshape(LEVELS * BW, group_cols), preferr...  6.06 us
    all_to_all x1, starting transfers between devices, body(): lax.all_to_all(regrouped, 'vec', split_axis=0, concat_axis=2, tiled=True)  5.45 us
    dot_general x1, matrix products, body(): jnp.einsum('lc,cbk->lbk', select, piece, preferred_element_type=jnp.float32)  3 us
    dot_general x1, matrix products, body(): lax.dot_general(interior_modes, interior_coef, contract, preferred_elemen...  2.9 us
  transfers between devices with their start and end apart: 3, of which 3 were waited for; matrix products, arithmetic and copies ran while one was open for 13% of the time, Pallas kernels for 0%

commit v1 on v0

--- a/solution.py
+++ b/solution.py
@@ -70,7 +70,10 @@
         interior_modes, interior_coef, contract, preferred_element_type=jnp.float32
     )
     my_ancestors = lax.dynamic_index_in_dim(ancestors, my_index, 0, keepdims=False)
-    piece = lax.all_gather(own_field[None], "sub", axis=0, tiled=True)
+    a0 = own_field[None]
+    piece = jnp.concatenate(
+        lax.all_to_all(jnp.stack(lax.axis_size("sub") * [a0], axis=0), "sub", 0, 0), axis=0
+    )
     labels = jnp.arange(piece.shape[0], dtype=jnp.int32)
     select = (my_ancestors[:, None] == labels[None, :]).astype(piece.dtype)
     ancestor_blocks = jnp.einsum(

time: 144 us -> 113 us (0.78)
  waiting for transfers between devices: 72 us -> 47.9 us
  between operations: 14.4 us -> 1 us
  starting transfers between devices: 16.4 us -> 21.1 us
  local copies, waits for them, and re-layouts: 22.5 us -> 24.3 us
    all_gather x1 -> x0, waiting for transfers between devices: 56.9 us -> none  [body(): piece = lax.all_gather(own_field[None], 'sub', axis=0, tiled=True)]
    all_to_all x0 -> x1, waiting for transfers between devices: none -> 32.5 us  [body(): lax.all_to_all(jnp.stack(lax.axis_size('sub') * [a0], axis=0), 'sub', 0, 0)]
    all_to_all x0 -> x1, starting transfers between devices: none -> 4.94 us  [body(): lax.all_to_all(jnp.stack(lax.axis_size('sub') * [a0], axis=0), 'sub', 0, 0)]
    another operation x1 -> x2, local copies, waits for them, and re-layouts: 0.74 us -> 2.52 us  [the longest x1 1.79 us: body(): jnp.stack(lax.axis_size('sub') * [a0], axis=0)]
    unnamed x16 -> x18, local copies, waits for them, and re-layouts: 17 us -> 17 us
  transfers between devices with their start and end apart: 3 -> 3, of which waited for: 3 -> 3; matrix products, arithmetic and copies ran while one was open for 13% -> 17% of each run, Pallas kernels for 0% -> 0%
where the time goes in v1:
time: 113 us; the launch traced here: 112 us
  waiting for transfers between devices  47.9 us (42%)
  local copies, waits for them, and re-layouts  24.3 us (22%)
  starting transfers between devices  21.1 us (19%)
  matrix products  12.7 us (11%)
  other arithmetic  4.63 us (4%)
    all_to_all x1, waiting for transfers between devices, body(): lax.all_to_all(jnp.stack(lax.axis_size('sub') * [a0], axis=0), 'sub', 0, 0)  32.5 us
    unnamed x18, local copies, waits for them, and re-layouts  17 us
    all_to_all x1, waiting for transfers between devices, body(): lax.all_to_all(picked, 'sub', split_axis=1, concat_axis=0, tiled=True)  12.7 us
    all_to_all x1, starting transfers between devices, body(): lax.all_to_all(picked, 'sub', split_axis=1, concat_axis=0, tiled=True)  10.8 us
    dot_general x1, matrix products, body(): jnp.dot(masked, ancestor_blocks.reshape(LEVELS * BW, group_cols), preferr...  6.06 us
    all_to_all x1, starting transfers between devices, body(): lax.all_to_all(regrouped, 'vec', split_axis=0, concat_axis=2, tiled=True)  5.45 us
    all_to_all x1, starting transfers between devices, body(): lax.all_to_all(jnp.stack(lax.axis_size('sub') * [a0], axis=0), 'sub', 0, 0)  4.94 us
    dot_general x1, matrix products, body(): jnp.einsum('lc,cbk->lbk', select, piece, preferred_element_type=jnp.float32)  3 us
  transfers between devices with their start and end apart: 3, of which 3 were waited for; matrix products, arithmetic and copies ran while one was open for 17% of the time, Pallas kernels for 0%

profile of v1, /device:TPU:8, one launch (start us, length us, event | category | flops | bytes accessed | tf_op | source)
XLA Modules:
  0.0 111.7 jit_solution(9008322832255128597)
XLA Ops:
  0.6 0.0 copy-start
  0.6 1.8 %reshape.101 = bf16[8,4,2560]{2,1,0:T(4,128)(2,1)} reshape(bf16[32,2560]{1,0:T(8,128)(2,1)} %param.7) | data formatting | bytes 327680 | tf_op jit(solution)/shard_map/reshape | solution.py:47
  2.4 5.4 %all-to-all-start = ((bf16[8,4,2560]{2,1,0:T(4,128)(2,1)}), bf16[8,4,2560]{2,1,0:T(4,128)(2,1)S(1)}, u32[]{:S(2)}, u32[]{:S(2)}) async-start(bf16[8,4,2560]{2,1,0:T(4,128)(2,1)} %reshape.101), calls=%async_computation | async-start | bytes 327680 | tf_op jit(solution)/shard_map/all_to_all | solution.py:48
  7.9 0.7 iota_compare_fusion
  8.6 0.7 copy.19
  9.4 0.1 reduce-window.9
  9.4 0.1 reduce
  9.5 0.7 and_compare_fusion.9
  10.2 2.7 %all-to-all-done = bf16[8,4,2560]{2,1,0:T(4,128)(2,1)S(1)} async-done(((bf16[8,4,2560]{2,1,0:T(4,128)(2,1)}), bf16[8,4,2560]{2,1,0:T(4,128)(2,1)S(1)}, u32[]{:S(2)}, u32[]{:S(2)}) %all-to-all-start) | async-done | bytes 163872 | tf_op jit(solution)/shard_map/all_to_all | solution.py:48
  12.9 0.8 slice_select_fusion.1
  13.8 0.1 reshape.103
  13.9 0.3 convolution_convert_fusion.1
  14.1 0.3 convolution_convert_fusion
  14.4 0.2 fusion.10
  14.6 0.2 fusion.11
  14.8 0.2 slice.64
  15.1 0.2 pad_select_fusion.7
  15.3 0.2 slice.65
  15.5 0.2 pad_select_fusion.6
  15.7 0.2 slice.66
  15.9 0.2 pad_select_fusion.5
  16.1 0.2 slice.67
  16.3 0.2 pad_select_fusion.4
  16.5 0.2 slice.68
  16.8 0.2 pad_select_fusion.3
  17.0 0.2 slice.69
  17.2 0.2 pad_select_fusion.2
  17.4 0.2 pad_select_fusion.1
  17.7 0.0 copy-start.2
  17.7 0.0 copy-start.3
  17.7 0.2 pad_select_fusion
  17.9 0.2 fusion.14
  18.1 0.9 copy.20
  19.0 10.8 %all-to-all-start.1 = ((bf16[4,32,1152]{2,0,1:T(4,128)(2,1)}), bf16[4,32,1152]{2,0,1:T(4,128)(2,1)S(1)}, u32[]{:S(2)}, u32[]{:S(2)}) async-start(bf16[4,32,1152]{2,0,1:T(4,128)(2,1)} %copy.20), calls=%async_computation.1 | async-start | bytes 589824 | tf_op jit(solution)/shard_map/all_to_all | solution.py:58
  29.7 12.7 %all-to-all-done.1 = bf16[4,32,1152]{2,0,1:T(4,128)(2,1)S(1)} async-done(((bf16[4,32,1152]{2,0,1:T(4,128)(2,1)}), bf16[4,32,1152]{2,0,1:T(4,128)(2,1)S(1)}, u32[]{:S(2)}, u32[]{:S(2)}) %all-to-all-start.1) | async-done | bytes 294944 | tf_op jit(solution)/shard_map/all_to_all | solution.py:58
  42.5 0.1 reshape.105
  42.6 0.0 copy-done
  42.6 0.2 convolution_convert_fusion.2
  42.7 0.0 copy-start.1
  42.8 1.8 %stack.3 = bf16[32,1,256,128]{3,2,1,0:T(8,128)(2,1)} broadcast(bf16[256,128]{1,0:T(8,128)(2,1)S(1)} %convolution_convert_fusion.2), dimensions={2,3} | broadcast | bytes 2162688 | tf_op jit(solution)/shard_map/stack | solution.py:75
  44.5 4.9 %all-to-all-start.2 = ((bf16[32,1,256,128]{3,2,1,0:T(8,128)(2,1)}), bf16[32,1,256,128]{3,2,1,0:T(8,128)(2,1)}, u32[]{:S(2)}, u32[]{:S(2)}) async-start(bf16[32,1,256,128]{3,2,1,0:T(8,128)(2,1)} %stack.3), calls=%async_computation.2 | async-start | bytes 4194304 | tf_op jit(solution)/shard_map/all_to_all | solution.py:75
  49.5 0.0 copy-done.2
  49.5 0.2 dynamic-slice_reduce_fusion
  49.7 0.0 copy-done.3
  49.7 0.5 mul.16
  50.2 0.0 copy-done.1
  50.2 6.8 %copy.29 = bf16[96,8,16,256]{3,1,2,0:T(8,128)(2,1)} copy(bf16[96,8,16,256]{3,2,1,0:T(8,128)(2,1)S(1)} %bitcast.57) | data formatting | bytes 12582912
  57.0 8.8 %copy.21 = bf16[4096,768]{0,1:T(8,128)(2,1)} copy(bf16[4096,768]{1,0:T(8,128)(2,1)} %param.12) | data formatting | bytes 12582912 | tf_op args[5]
  65.8 32.5 %all-to-all-done.2 = bf16[32,1,256,128]{3,2,1,0:T(8,128)(2,1)} async-done(((bf16[32,1,256,128]{3,2,1,0:T(8,128)(2,1)}), bf16[32,1,256,128]{3,2,1,0:T(8,128)(2,1)}, u32[]{:S(2)}, u32[]{:S(2)}) %all-to-all-start.2) | async-done | bytes 2097184 | tf_op jit(solution)/shard_map/all_to_all | solution.py:75
  98.3 0.0 slice-start
  98.3 3.0 %fusion.7 = bf16[3,256,128]{2,0,1:T(4,128)(2,1)S(1)} fusion(bf16[32,1,256,128]{3,2,1,0:T(8,128)(2,1)} %all-to-all-done.2, s32[3]{0:T(128)S(1)} %dynamic-slice_reduce_fusion), kind=kOutput, calls=%fused_computation.10 | convolution fusion | flops 6389856 | bytes 2293772 | tf_op jit(solution)/shard_map/lc,cbk->lbk/dot_general | solution.py:79
  101.4 0.0 slice-start.1
  101.4 6.1 %fusion = f32[4096,128]{0,1:T(8,128)S(1)} fusion(bf16[768,128]{1,0:T(8,128)(2,1)S(1)} %bitcast.61, bf16[4096,768]{0,1:T(8,128)(2,1)} %copy.21, bf16[4096,768]{0,1:T(8,128)(2,1)} %bitcast.56), kind=kOutput, calls=%fused_computation | convolution fusion | flops 808452096 | bytes 14876672 | tf_op jit(solution)/shard_map/dot_general | solution.py:87
  107.4 0.0 slice-done
  107.5 0.0 slice-done.1
  107.5 2.9 %fusion.3 = bf16[4096,128]{0,1:T(8,128)(2,1)S(1)} fusion(f32[4096,128]{0,1:T(8,128)S(1)} %fusion, bf16[4096,1024]{1,0:T(8,128)(2,1)S(1)} %bitcast.59, bf16[128,1152]{1,0:T(8,128)(2,1)S(1)} %reshape.105), kind=kOutput, calls=%fused_computation.4 | convolution fusion | flops 1074790400 | bytes 11796480 | tf_op jit(solution)/shard_map/dot_general | solution.py:69
  110.4 1.3 %copy.25 = bf16[4096,128]{1,0:T(8,128)(2,1)} copy(bf16[4096,128]{0,1:T(8,128)(2,1)S(1)} %fusion.3) | data formatting | bytes 2097152
  (12 shorter events, 0.2 us)
Async XLA Ops:
  0.6 41.9 %copy-start = (bf16[8192,128]{1,0:T(8,128)(2,1)S(1)}, bf16[8192,128]{1,0:T(8,128)(2,1)}, u32[]{:S(2)}) copy-start(bf16[8192,128]{1,0:T(8,128)(2,1)} %param.11) | copy-start | bytes 6291460
  2.4 10.5 %all-to-all-start = ((bf16[8,4,2560]{2,1,0:T(4,128)(2,1)}), bf16[8,4,2560]{2,1,0:T(4,128)(2,1)S(1)}, u32[]{:S(2)}, u32[]{:S(2)}) async-start(bf16[8,4,2560]{2,1,0:T(4,128)(2,1)} %reshape.101), calls=%async_computation | async-start | bytes 327680 | tf_op jit(solution)/shard_map/all_to_all | solution.py:48
  17.7 31.8 %copy-start.2 = (s32[32,3]{0,1:T(4,128)S(1)}, s32[32,3]{0,1:T(4,128)}, u32[]{:S(2)}) copy-start(s32[32,3]{0,1:T(4,128)} %param.9) | copy-start | bytes 1156
  17.7 32.0 %copy-start.3 = (s32[1,16,3]{1,0,2:T(1,128)S(1)}, s32[1,16,3]{1,0,2:T(1,128)}, u32[]{:S(2)}) copy-start(s32[1,16,3]{1,0,2:T(1,128)} %param.13) | copy-start | bytes 580
  19.0 23.5 %all-to-all-start.1 = ((bf16[4,32,1152]{2,0,1:T(4,128)(2,1)}), bf16[4,32,1152]{2,0,1:T(4,128)(2,1)S(1)}, u32[]{:S(2)}, u32[]{:S(2)}) async-start(bf16[4,32,1152]{2,0,1:T(4,128)(2,1)} %copy.20), calls=%async_computation.1 | async-start | bytes 589824 | tf_op jit(solution)/shard_map/all_to_all | solution.py:58
  42.7 7.5 %copy-start.1 = (bf16[256,128]{1,0:T(8,128)(2,1)}, bf16[256,128]{1,0:T(8,128)(2,1)S(1)}, u32[]{:S(2)}) copy-start(bf16[256,128]{1,0:T(8,128)(2,1)S(1)} %convolution_convert_fusion.2) | copy-start | bytes 196612
  44.5 53.8 %all-to-all-start.2 = ((bf16[32,1,256,128]{3,2,1,0:T(8,128)(2,1)}), bf16[32,1,256,128]{3,2,1,0:T(8,128)(2,1)}, u32[]{:S(2)}, u32[]{:S(2)}) async-start(bf16[32,1,256,128]{3,2,1,0:T(8,128)(2,1)} %stack.3), calls=%async_computation.2 | async-start | bytes 4194304 | tf_op jit(solution)/shard_map/all_to_all | solution.py:75
  98.3 9.1 %slice-start = ((s8[8388608]{0:T(1024)(128)(4,1)}), s8[4194304]{0:T(1024)(128)(4,1)S(1)}, s32[]{:S(2)}) async-start(s8[8388608]{0:T(1024)(128)(4,1)} %bitcast.58), calls=%async_computation.3 | async-start | bytes 8388608
  101.4 6.1 %slice-start.1 = ((s8[8388608]{0:T(1024)(128)(4,1)}), s8[4194304]{0:T(1024)(128)(4,1)S(1)}, s32[]{:S(2)}) async-start(s8[8388608]{0:T(1024)(128)(4,1)} %bitcast.58), calls=%async_computation.4 | async-start | bytes 8388608
